TPU v7x, 256 devices: a whole 4x4x8 slice. The times are simulated.
256 devices in a mesh: dp: 16 (over z, core), frame: 16 (over x, y).
Axes of the slice: x: 4, y: 4, z: 8, core: 2. Of those that a mesh axis runs over, the one named last changes fastest.
Arguments:
- latents: bfloat16 [16, 32, 128, 1280], P('dp', 'frame'), may hold values from -330 to 330
- timestep: int32 [16], P('dp'), may hold values from 0 to 999
- norm_gain: float32 [1280], replicated, may hold values from 0.1 to 1.9
- time_weight: bfloat16 [320, 1280], P('dp'), may hold values from -0.3125 to 0.3125
- conv_weight: bfloat16 [3, 1280, 1280], P(None, ('dp', 'frame')), may hold values from -0.09375 to 0.09375
- attend_weight: bfloat16 [1280, 3840], P(('dp', 'frame')), may hold values from -0.3354102 to 0.3354102
- output_weight: bfloat16 [1280, 1280], P(('dp', 'frame')), may hold values from -0.15625 to 0.15625
Outputs:
- block_out: bfloat16 [16, 32, 128, 1280], P('dp', 'frame')
All inputs are finite; a program needn't handle non-finite values.
Results may differ from a plain program's by a relative error of at most 0.0051.
Values may be sent and summed in bfloat16 or wider, within the bound.
No kernel may reach another device: no remote copies, remote signals or barrier semaphores. Data moves between devices by JAX's collectives and lax.ppermute only.
A program may use at most 128 MiB of HBM per device.

v0:
```python
import functools
import math
import jax
import jax.numpy as jnp
from jax import lax
from jax.sharding import Mesh
from jax.sharding import PartitionSpec as P

HEADS = 20
HD = 64
GROUPS = 32
TEMB = 320
FRAME = ("frame_0", "frame_1")
DP_FRAME = ("dp", "frame_0", "frame_1")


def laid_out(blocks, dim):
    blocks = jnp.moveaxis(blocks, 0, dim)
    dims = blocks.shape
    return blocks.reshape(*dims[:dim], dims[dim] * dims[dim + 1], *dims[dim + 2 :])


def sent_to_all(array, axis):
    count = lax.axis_size(axis)
    return lax.all_to_all(
        jnp.broadcast_to(array[None], (count, *array.shape)), axis, 0, 0, tiled=True
    )


def collect(array, axis, dim):
    return laid_out(sent_to_all(array, axis), dim)


def by_axis(array, axes):
    return functools.reduce(lax.psum, axes, array)


def with_halo(array, sides, width):
    for axis, dim in sides:
        count, length = (lax.axis_size(axis), array.shape[dim])
        up = [(i, (i + 1) % count) for i in range(count - 1)]
        down = [(j, i) for i, j in up]
        last = lax.slice_in_dim(array, length - width, length, axis=dim)
        initial = lax.slice_in_dim(array, 0, width, axis=dim)
        before = lax.ppermute(last, axis, up)
        after = lax.ppermute(initial, axis, down)
        array = jnp.concatenate([before, array, after], axis=dim)
    return array


def sinusoid(timestep):
    half_dim = TEMB // 2
    ladder = jnp.arange(half_dim, dtype=jnp.float32)
    freqs = jnp.exp(-math.log(10000.0) * ladder / half_dim)
    angles = timestep.astype(jnp.float32)[:, None] * freqs[None, :]
    return jnp.concatenate([jnp.cos(angles), jnp.sin(angles)], axis=-1)


def attend_pixels(triple):
    count_items, frames_all, pixels_here, width_three = triple.shape
    channels = width_three // 3
    parts = triple.reshape(count_items, frames_all, pixels_here, 3, HEADS, HD)
    queries = parts[:, :, :, 0]
    key_part = parts[:, :, :, 1]
    value_part = parts[:, :, :, 2]
    scores = jnp.einsum(
        "nfphd,ngphd->nphfg", queries, key_part, preferred_element_type=jnp.float32
    ) / math.sqrt(HD)
    peak = jnp.max(scores, axis=-1, keepdims=True)
    expo = jnp.exp(scores - peak)
    probs = (expo / jnp.sum(expo, axis=-1, keepdims=True)).astype(jnp.bfloat16)
    attended = jnp.einsum(
        "nphfg,ngphd->nfphd", probs, value_part, preferred_element_type=jnp.float32
    )
    attended = attended.astype(jnp.bfloat16).reshape(count_items, frames_all, pixels_here, channels)
    return lax.all_to_all(attended, FRAME, split_axis=1, concat_axis=2, tiled=True)


def fold_rows(total, rows, piece):
    return total + jnp.dot(rows, piece, preferred_element_type=jnp.float32)


def shards(latents, timestep, norm_gain, time_weight, conv_weight, attend_weight, output_weight):
    count_clips, frames_dev, pixels, channels = latents.shape
    group_width = channels // GROUPS
    time_full = collect(time_weight, "dp", 0)
    features = sinusoid(timestep).astype(jnp.bfloat16)
    time_bias = jnp.dot(features, time_full, preferred_element_type=jnp.float32)
    values = latents.astype(jnp.float32)
    grouped = values.reshape(count_clips, frames_dev, pixels, GROUPS, group_width)
    members = frames_dev * lax.axis_size(FRAME) * pixels * group_width
    center = by_axis(jnp.sum(grouped, axis=(1, 2, 4)), FRAME) / members
    deviate = grouped - center[:, None, None, :, None]
    spread = by_axis(jnp.sum(deviate * deviate, axis=(1, 2, 4)), FRAME) / members
    normed_group = deviate / jnp.sqrt(spread[:, None, None, :, None] + 1e-05)
    scaled = normed_group.reshape(count_clips, frames_dev, pixels, channels) * norm_gain
    hidden = jax.nn.silu(scaled).astype(jnp.bfloat16)
    padded = with_halo(hidden, ((FRAME, 1),), 1)
    windows = [padded[:, offset : offset + frames_dev].reshape(-1, channels) for offset in range(3)]
    conv_init = jnp.zeros((count_clips * frames_dev * pixels, channels), jnp.float32)
    conv_slab = collect(conv_weight, FRAME, 1)
    total = conv_init
    piece = lax.all_gather(conv_slab, "dp", axis=1, tiled=True)
    for offset in range(3):
        total = fold_rows(total, windows[offset], piece[offset])
    conv = total
    conv = conv.reshape(count_clips, frames_dev, pixels, channels) + time_bias[:, None, None, :]
    residual = (values + conv).astype(jnp.bfloat16)
    rows = residual.astype(jnp.float32)
    row_mean = jnp.mean(rows, axis=-1, keepdims=True)
    row_var = jnp.mean((rows - row_mean) ** 2, axis=-1, keepdims=True)
    normed = ((rows - row_mean) / jnp.sqrt(row_var + 1e-05)).astype(jnp.bfloat16)
    attend_slab = collect(attend_weight, FRAME, 0)
    block = lax.all_to_all(normed, FRAME, split_axis=2, concat_axis=1, tiled=True)
    count_items, frames_all, pixels_here, width = block.shape
    flat = block.reshape(-1, width)
    empty = jnp.zeros((flat.shape[0], 3 * channels), jnp.float32)
    product = fold_rows(empty, flat, lax.all_gather(attend_slab, "dp", axis=0, tiled=True))
    triple_block = product.astype(jnp.bfloat16).reshape(
        count_items, frames_all, pixels_here, 3 * width
    )
    attended = attend_pixels(triple_block)
    flat_attended = attended.reshape(-1, channels)
    output_slab = collect(output_weight, FRAME, 0)
    out_init = jnp.zeros((flat_attended.shape[0], channels), jnp.float32)
    projected = fold_rows(
        out_init, flat_attended, lax.all_gather(output_slab, "dp", axis=0, tiled=True)
    )
    mixed = rows + projected.reshape(count_clips, frames_dev, pixels, channels)
    return mixed.astype(jnp.bfloat16)


def solution(mesh):
    split = Mesh(mesh.devices.reshape(mesh.shape["dp"], 4, 4), ("dp", "frame_0", "frame_1"))
    placed = (
        P("dp", FRAME, None, None),
        P("dp"),
        P(),
        P("dp", None),
        P(None, DP_FRAME, None),
        P(DP_FRAME, None),
        P(DP_FRAME, None),
    )
    return jax.shard_map(
        shards, mesh=split, in_specs=placed, out_specs=P("dp", FRAME, None, None), check_vma=False
    )
```

profile of v0, /device:TPU:1, one launch (start us, length us, event | category | flops | bytes accessed | tf_op | source)
XLA Modules:
  0.0 227.9 jit_solution(3048187557169434955)
XLA Ops:
  6.5 1.0 broadcast_in_dim.8
  7.6 21.1 %all_to_all.50 = bf16[16,3,5,1280]{3,1,2,0:T(4,128)(2,1)S(1)} all-to-all(bf16[16,3,5,1280]{3,1,2,0:T(4,128)(2,1)S(1)} %broadcast_in_dim.8), channel_id=1, replica_groups=mesh['dp'=16,'frame_0'=4,'frame_1'=4] {'frame_0','frame_1'}, dimensions={0} | all-to-all | bytes 1228800 | tf_op jit(solution)/shard_map/all_to_all | solution.py:25
  29.8 17.6 %all_to_all.51 = bf16[16,5,3840]{2,1,0:T(8,128)(2,1)S(1)} all-to-all(bf16[16,5,3840]{2,1,0:T(8,128)(2,1)S(1)} %broadcast_in_dim.10), channel_id=1, replica_groups=mesh['dp'=16,'frame_0'=4,'frame_1'=4] {'frame_0','frame_1'}, dimensions={0} | all-to-all | bytes 1228800 | tf_op jit(solution)/shard_map/all_to_all | solution.py:25
  47.4 1.1 reshape.187
  49.3 3.5 %all-to-all-start.5 = ((bf16[16,5,1280]{2,1,0:T(8,128)(2,1)}), bf16[16,5,1280]{2,1,0:T(8,128)(2,1)S(1)}, u32[]{:S(2)}, u32[]{:S(2)}) async-start(bf16[16,5,1280]{2,1,0:T(8,128)(2,1)} %broadcast_in_dim.11), calls=%async_computation.5 | async-start | bytes 655360 | tf_op jit(solution)/shard_map/all_to_all | solution.py:25
  53.2 9.3 %psum.28 = f32[1,32]{1,0:T(1,128)S(1)} all-reduce(f32[1,32]{1,0:T(1,128)S(1)} %bitcast.84), channel_id=1, replica_groups=mesh['dp'=16,'frame_0'=4,'frame_1'=4] {'frame_0'}, use_global_device_ids=true, to_apply=%region_2.0 | all-reduce | flops 32 | bytes 256 | tf_op jit(solution)/shard_map/psum | solution.py:35
  62.5 9.2 %psum.29 = f32[1,32]{1,0:T(1,128)S(1)} all-reduce(f32[1,32]{1,0:T(1,128)S(1)} %psum.28), channel_id=1, replica_groups=mesh['dp'=16,'frame_0'=4,'frame_1'=4] {'frame_1'}, use_global_device_ids=true, to_apply=%region_3.0 | all-reduce | flops 32 | bytes 256 | tf_op jit(solution)/shard_map/psum | solution.py:35
  72.3 6.8 %psum.30 = f32[1,32]{1,0:T(1,128)S(1)} all-reduce(f32[1,32]{1,0:T(1,128)S(1)} %bitcast.83), channel_id=1, replica_groups=mesh['dp'=16,'frame_0'=4,'frame_1'=4] {'frame_0'}, use_global_device_ids=true, to_apply=%region_6.7 | all-reduce | flops 32 | bytes 256 | tf_op jit(solution)/shard_map/psum | solution.py:35
  79.1 6.8 %psum.31 = f32[1,32]{1,0:T(1,128)S(1)} all-reduce(f32[1,32]{1,0:T(1,128)S(1)} %psum.30), channel_id=1, replica_groups=mesh['dp'=16,'frame_0'=4,'frame_1'=4] {'frame_1'}, use_global_device_ids=true, to_apply=%region_7.8 | all-reduce | flops 32 | bytes 256 | tf_op jit(solution)/shard_map/psum | solution.py:35
  87.1 16.0 %all-to-all-start.1 = ((bf16[16,20,1280]{2,1,0:T(8,128)(2,1)}), bf16[16,20,1280]{2,1,0:T(8,128)(2,1)S(1)}, u32[]{:S(2)}, u32[]{:S(2)}) async-start(bf16[16,20,1280]{2,1,0:T(8,128)(2,1)} %broadcast_in_dim.9), calls=%async_computation.1 | async-start | bytes 1966080 | tf_op jit(solution)/shard_map/all_to_all | solution.py:25
  104.3 3.6 %collective-permute-start = (bf16[1,1,128,1280]{3,2,1,0:T(8,128)(2,1)}, bf16[1,1,128,1280]{3,2,1,0:T(8,128)(2,1)S(1)}, u32[]{:S(2)}, u32[]{:S(2)}) collective-permute-start(bf16[1,1,128,1280]{3,2,1,0:T(8,128)(2,1)} %get-tuple-element.12), channel_id=1, source_target_pairs={{0,1},{1,2},{2,3},{3,4},{4,5},{5,6},{6,7},{7,8},{8,9},{9,10},{10,1... | collective-permute-start | bytes 983048 | tf_op jit(solution)/shard_map/ppermute | solution.py:45
  108.0 1.3 collective-permute-start.1
  110.9 4.4 %collective-permute-done = bf16[1,1,128,1280]{3,2,1,0:T(8,128)(2,1)S(1)} collective-permute-done((bf16[1,1,128,1280]{3,2,1,0:T(8,128)(2,1)}, bf16[1,1,128,1280]{3,2,1,0:T(8,128)(2,1)S(1)}, u32[]{:S(2)}, u32[]{:S(2)}) %collective-permute-start) | collective-permute-done | bytes 327712 | tf_op jit(solution)/shard_map/ppermute | solution.py:45
  115.2 3.6 %collective-permute-done.1 = bf16[1,1,128,1280]{3,2,1,0:T(8,128)(2,1)} collective-permute-done((bf16[1,1,128,1280]{3,2,1,0:T(8,128)(2,1)S(1)}, bf16[1,1,128,1280]{3,2,1,0:T(8,128)(2,1)}, u32[]{:S(2)}, u32[]{:S(2)}) %collective-permute-start.1) | collective-permute-done | bytes 327712 | tf_op jit(solution)/shard_map/ppermute | solution.py:46
  118.9 2.1 pad_maximum_fusion.1
  121.0 17.5 %all-to-all-done.1 = bf16[16,20,1280]{2,1,0:T(8,128)(2,1)S(1)} async-done(((bf16[16,20,1280]{2,1,0:T(8,128)(2,1)}), bf16[16,20,1280]{2,1,0:T(8,128)(2,1)S(1)}, u32[]{:S(2)}, u32[]{:S(2)}) %all-to-all-start.1) | async-done | bytes 819232 | tf_op jit(solution)/shard_map/all_to_all | solution.py:25
  139.0 3.2 %fusion.1 = f32[256,1280]{1,0:T(8,128)S(1)} fusion(bf16[256,1280]{1,0:T(8,128)(2,1)} %bitcast.80, bf16[3,1280,1280]{2,1,0:T(8,128)(2,1)} %all-gather.4.cloned.1.call-done), kind=kOutput, calls=%fused_computation.3 | convolution fusion | flops 838860800 | bytes 5242880 | tf_op jit(solution)/shard_map/dot_general | solution.py:80
  142.2 3.0 %fusion.2 = f32[256,1280]{1,0:T(8,128)S(1)} fusion(bf16[256,1280]{1,0:T(8,128)(2,1)S(1)} %bitcast.75, bf16[3,1280,1280]{2,1,0:T(8,128)(2,1)} %all-gather.4.cloned.1.call-done), kind=kOutput, calls=%fused_computation.5 | convolution fusion | flops 838860800 | bytes 5242880 | tf_op jit(solution)/shard_map/dot_general | solution.py:80
  145.2 3.0 %fusion.7 = f32[256,1280]{1,0:T(8,128)S(1)} fusion(f32[256,1280]{1,0:T(8,128)S(1)} %fusion.1, f32[256,1280]{1,0:T(8,128)S(1)} %fusion.2, bf16[256,1280]{1,0:T(8,128)(2,1)S(1)} %bitcast.79, bf16[3,1280,1280]{2,1,0:T(8,128)(2,1)} %all-gather.4.cloned.1.call-done), kind=kOutput, calls=%fused_computation.11 | convolution fusion | flops 839516160 | bytes 7864320 | tf_op jit(solution)/shard_map/dot_general | solution.py:80
  149.8 17.2 %all_to_all.52 = bf16[1,2,128,1280]{3,1,0,2:T(2,128)(2,1)S(1)} all-to-all(bf16[1,2,128,1280]{3,1,0,2:T(2,128)(2,1)S(1)} %copy.42), channel_id=1, replica_groups=mesh['dp'=16,'frame_0'=4,'frame_1'=4] {'frame_0','frame_1'}, dimensions={2} | all-to-all | bytes 1310720 | tf_op jit(solution)/shard_map/all_to_all | solution.py:114
  168.0 8.1 %all-gather.6.cloned.1.call-done = bf16[1280,3840]{1,0:T(8,128)(2,1)} async-done(((bf16[80,3840]{1,0:T(8,128)(2,1)}), bf16[1280,3840]{1,0:T(8,128)(2,1)}) %all-gather.6.cloned.1.call-update) | async-done | bytes 9830416 | tf_op jit(solution)/shard_map/all_gather | solution.py:118
  176.1 6.7 %convolution_convert_fusion = bf16[256,3840]{1,0:T(8,128)(2,1)S(1)} fusion(bf16[256,1280]{1,0:T(8,128)(2,1)} %bitcast.82, bf16[1280,3840]{1,0:T(8,128)(2,1)} %all-gather.6.cloned.1.call-done), kind=kOutput, calls=%fused_computation.1 | convolution fusion | flops 2517565440 | bytes 12451840 | tf_op jit(solution)/shard_map/dot_general | solution.py:80
  182.8 4.5 %reshape_reshape.3 = bf16[1,32,8,3,20,64]{5,4,3,2,1,0:T(8,128)(2,1)} reshape(bf16[256,3840]{1,0:T(8,128)(2,1)S(1)} %convolution_convert_fusion) | data formatting | bytes 3932160 | tf_op jit(solution)/shard_map/reshape;reshape | solution.py:62
  187.3 3.3 %fusion.37 = (bf16[1,32,8,1,20,64]{5,4,3,2,1,0:T(8,128)(2,1)S(1)}, bf16[1,32,8,1,20,64]{5,4,3,2,1,0:T(8,128)(2,1)S(1)}, bf16[1,32,8,1,20,64]{5,4,3,2,1,0:T(8,128)(2,1)S(1)}) fusion(bf16[1,32,8,3,20,64]{5,4,3,2,1,0:T(8,128)(2,1)} %reshape_reshape.3), kind=kLoop, calls=%fused_computation.57 | loop fusion | bytes 3932160 | tf_op jit(solution)/shard_map/slice | solution.py:65
  190.5 1.7 fusion.30
  192.3 6.0 %fusion.39 = (f32[8,20,32]{2,1,0:T(8,128)S(1)}, f32[8,20,32,32]{2,3,1,0:T(8,128)S(1)}) fusion(f32[8,20,32,32]{2,3,1,0:T(8,128)S(1)} %fusion.30), kind=kOutput, calls=%fused_computation.59 | output fusion | flops 655391 | bytes 1331200 | tf_op jit(solution)/shard_map/sub | solution.py:70
  198.2 1.2 fusion.24
  200.0 1.6 reshape.191
  201.7 4.6 %all-to-all-start.4 = ((bf16[1,32,8,1280]{3,2,0,1:T(8,128)(2,1)}), bf16[1,32,8,1280]{3,2,0,1:T(8,128)(2,1)S(1)}, u32[]{:S(2)}, u32[]{:S(2)}) async-start(bf16[1,32,8,1280]{3,2,0,1:T(8,128)(2,1)} %bitcast.22), calls=%async_computation.4 | async-start | bytes 1310720 | tf_op jit(solution)/shard_map/all_to_all | solution.py:76
  206.2 9.3 %all-gather.8.cloned.1.call-done = bf16[1280,1280]{1,0:T(8,128)(2,1)} async-done(((bf16[80,1280]{1,0:T(8,128)(2,1)}), bf16[1280,1280]{1,0:T(8,128)(2,1)}) %all-gather.8.cloned.1.call-update) | async-done | bytes 3276816 | tf_op jit(solution)/shard_map/all_gather | solution.py:127
  215.6 2.0 all-to-all-done.4
  217.6 3.8 %fusion.14 = bf16[1,2,128,1280]{3,2,1,0:T(8,128)(2,1)} fusion(bf16[1280,1280]{1,0:T(8,128)(2,1)} %all-gather.8.cloned.1.call-done, bf16[1,2,128,1280]{3,2,1,0:T(8,128)(2,1)S(1)} %get-tuple-element.6, bf16[1,2,16,8,1280]{4,3,1,2,0:T(8,128)(2,1)S(1)} %bitcast.81), kind=kOutput, calls=%fused_computation.16 | convolution fusion | flops 839843840 | bytes 5242880 | tf_op jit(solution)/shard_map/dot_general | solution.py:80
  (53 shorter events, 9.5 us)
Async XLA Ops:
  6.5 132.4 %all-gather.4.cloned.1.call-start = ((), (), s32[]{:S(2)}) async-start(), calls=%async_computation.6 | async-start | bytes 10444800 | tf_op jit(solution)/shard_map/all_gather | solution.py:103
  7.6 22.1 %copy-start.2 = (bf16[5,3840]{1,0:T(8,128)(2,1)S(1)}, bf16[5,3840]{1,0:T(8,128)(2,1)}, u32[]{:S(2)}) copy-start(bf16[5,3840]{1,0:T(8,128)(2,1)} %param.12) | copy-start | bytes 115204
  29.6 146.4 %all-gather.6.cloned.1.call-start = ((), (), s32[]{:S(2)}) async-start(), calls=%async_computation.7 | async-start | bytes 10444800 | tf_op jit(solution)/shard_map/all_gather | solution.py:118
  47.4 1.1 copy-start.4
  47.4 5.4 %copy-start = (bf16[1,2,128,1280]{3,2,1,0:T(8,128)(2,1)S(1)}, bf16[1,2,128,1280]{3,2,1,0:T(8,128)(2,1)}, u32[]{:S(2)}) copy-start(bf16[1,2,128,1280]{3,2,1,0:T(8,128)(2,1)} %param.7) | copy-start | bytes 1966084
  48.5 37.6 %copy-start.3 = (bf16[20,1280]{1,0:T(8,128)(2,1)S(1)}, bf16[20,1280]{1,0:T(8,128)(2,1)}, u32[]{:S(2)}) copy-start(bf16[20,1280]{1,0:T(8,128)(2,1)} %param.10) | copy-start | bytes 153604
  49.3 36.8 %all-to-all-start.5 = ((bf16[16,5,1280]{2,1,0:T(8,128)(2,1)}), bf16[16,5,1280]{2,1,0:T(8,128)(2,1)S(1)}, u32[]{:S(2)}, u32[]{:S(2)}) async-start(bf16[16,5,1280]{2,1,0:T(8,128)(2,1)} %broadcast_in_dim.11), calls=%async_computation.5 | async-start | bytes 655360 | tf_op jit(solution)/shard_map/all_to_all | solution.py:25
  72.1 31.0 %copy-start.5 = (f32[1280]{0:T(1024)S(1)}, f32[1280]{0:T(1024)}, u32[]{:S(2)}) copy-start(f32[1280]{0:T(1024)} %param.9) | copy-start | bytes 15364
  87.1 51.4 %all-to-all-start.1 = ((bf16[16,20,1280]{2,1,0:T(8,128)(2,1)}), bf16[16,20,1280]{2,1,0:T(8,128)(2,1)S(1)}, u32[]{:S(2)}, u32[]{:S(2)}) async-start(bf16[16,20,1280]{2,1,0:T(8,128)(2,1)} %broadcast_in_dim.9), calls=%async_computation.1 | async-start | bytes 1966080 | tf_op jit(solution)/shard_map/all_to_all | solution.py:25
  103.1 112.5 %all-gather.8.cloned.1.call-start = ((), (), s32[]{:S(2)}) async-start(), calls=%async_computation.8 | async-start | bytes 3481600 | tf_op jit(solution)/shard_map/all_gather | solution.py:127
  104.3 10.9 %collective-permute-start = (bf16[1,1,128,1280]{3,2,1,0:T(8,128)(2,1)}, bf16[1,1,128,1280]{3,2,1,0:T(8,128)(2,1)S(1)}, u32[]{:S(2)}, u32[]{:S(2)}) collective-permute-start(bf16[1,1,128,1280]{3,2,1,0:T(8,128)(2,1)} %get-tuple-element.12), channel_id=1, source_target_pairs={{0,1},{1,2},{2,3},{3,4},{4,5},{5,6},{6,7},{7,8},{8,9},{9,10},{10,1... | collective-permute-start | bytes 983048 | tf_op jit(solution)/shard_map/ppermute | solution.py:45
  108.0 10.9 %collective-permute-start.1 = (bf16[1,1,128,1280]{3,2,1,0:T(8,128)(2,1)S(1)}, bf16[1,1,128,1280]{3,2,1,0:T(8,128)(2,1)}, u32[]{:S(2)}, u32[]{:S(2)}) collective-permute-start(bf16[1,1,128,1280]{3,2,1,0:T(8,128)(2,1)S(1)} %get-tuple-element.13), channel_id=1, source_target_pairs={{1,0},{2,1},{3,2},{4,3},{5,4},{6,5},{7,6},{8,7},{9,8},{10,9},{11,1... | collective-permute-start | bytes 983048 | tf_op jit(solution)/shard_map/ppermute | solution.py:46
  142.2 3.0 %copy-start.1 = (bf16[1,2,128,1280]{3,2,1,0:T(8,128)(2,1)S(1)}, bf16[1,2,128,1280]{3,2,1,0:T(8,128)(2,1)}, u32[]{:S(2)}) copy-start(bf16[1,2,128,1280]{3,2,1,0:T(8,128)(2,1)} %get-tuple-element.10) | copy-start | bytes 1966084
  201.7 15.9 %all-to-all-start.4 = ((bf16[1,32,8,1280]{3,2,0,1:T(8,128)(2,1)}), bf16[1,32,8,1280]{3,2,0,1:T(8,128)(2,1)S(1)}, u32[]{:S(2)}, u32[]{:S(2)}) async-start(bf16[1,32,8,1280]{3,2,0,1:T(8,128)(2,1)} %bitcast.22), calls=%async_computation.4 | async-start | bytes 1310720 | tf_op jit(solution)/shard_map/all_to_all | solution.py:76
Sparse Core Ops, SparseCore 0:
  29.8 63.7 all-gather.3
  95.4 80.5 all-gather.5
  177.9 37.6 all-gather.7
where the time goes:
time: 229 us; the launch traced here: 228 us
  blocking collectives  88 us (38%)
  waiting for transfers between devices  45.1 us (20%)
  starting transfers between devices  29.1 us (13%)
  matrix products  23 us (10%)
  local copies, waits for them, and re-layouts  18.6 us (8%)
  between operations  14 us (6%)
  other arithmetic  10.1 us (4%)
    all_to_all x2, blocking collectives, sent_to_all(): lax.all_to_all(jnp.broadcast_to(array[None], (count, *array.shape)), axis...  38.7 us
    psum x4, blocking collectives, by_axis(): return functools.reduce(lax.psum, axes, array)  32.1 us
    dot_general x5, matrix products, fold_rows(): return total + jnp.dot(rows, piece, preferred_element_type=jnp.float32)  19.8 us
    all_to_all x2, starting transfers between devices, sent_to_all(): lax.all_to_all(jnp.broadcast_to(array[None], (count, *array.shape)), axis...  19.5 us
    all_to_all x2, waiting for transfers between devices, sent_to_all(): lax.all_to_all(jnp.broadcast_to(array[None], (count, *array.shape)), axis...  17.5 us
    all_to_all x1, blocking collectives, shards(): lax.all_to_all(normed, FRAME, split_axis=2, concat_axis=1, tiled=True)  17.2 us
    all_gather x1, waiting for transfers between devices, shards(): lax.all_gather(output_slab, 'dp', axis=0, tiled=True)  9.34 us
    all_gather x1, waiting for transfers between devices, shards(): lax.all_gather(attend_slab, 'dp', axis=0, tiled=True)  8.12 us
  transfers between devices with their start and end apart: 8, of which 6 were waited for; matrix products, arithmetic and copies ran while one was open for 20% of the time, Pallas kernels for 0%

commit v1 on v0

--- a/solution.py
+++ b/solution.py
@@ -124,7 +124,11 @@
     output_slab = collect(output_weight, FRAME, 0)
     out_init = jnp.zeros((flat_attended.shape[0], channels), jnp.float32)
     projected = fold_rows(
-        out_init, flat_attended, lax.all_gather(output_slab, "dp", axis=0, tiled=True)
+        out_init,
+        flat_attended,
+        jnp.concatenate(
+            lax.all_to_all(jnp.stack([output_slab] * lax.axis_size("dp")), "dp", 0, 0), axis=0
+        ),
     )
     mixed = rows + projected.reshape(count_clips, frames_dev, pixels, channels)
     return mixed.astype(jnp.bfloat16)

time: 229 us -> 287 us (1.25)
  the two profiles are of different devices: /device:TPU:1 before, /device:TPU:96 now
where the time goes in v1:
time: 287 us; the launch traced here: 286 us
  blocking collectives  106 us (37%)
  waiting for transfers between devices  81.4 us (28%)
  starting transfers between devices  33.9 us (12%)
  matrix products  23.1 us (8%)
  local copies, waits for them, and re-layouts  18.4 us (6%)
  between operations  14.3 us (5%)
  other arithmetic  9.09 us (3%)
    all_gather x1, waiting for transfers between devices, shards(): lax.all_gather(attend_slab, 'dp', axis=0, tiled=True)  63.8 us
    all_to_all x2, blocking collectives, sent_to_all(): lax.all_to_all(jnp.broadcast_to(array[None], (count, *array.shape)), axis...  39.9 us
    psum x4, blocking collectives, by_axis(): return functools.reduce(lax.psum, axes, array)  34.9 us
    all_to_all x1, blocking collectives, attend_pixels(): lax.all_to_all(attended, FRAME, split_axis=1, concat_axis=2, tiled=True)  31.3 us
    dot_general x5, matrix products, fold_rows(): return total + jnp.dot(rows, piece, preferred_element_type=jnp.float32)  19.9 us
    all_to_all x2, starting transfers between devices, sent_to_all(): lax.all_to_all(jnp.broadcast_to(array[None], (count, *array.shape)), axis...  15.3 us
    all_to_all x1, waiting for transfers between devices, shards(): lax.all_to_all(normed, FRAME, split_axis=2, concat_axis=1, tiled=True)  10.7 us
    all_to_all x1, starting transfers between devices, shards(): lax.all_to_all(jnp.stack([output_slab] * lax.axis_size('dp')), 'dp', 0, 0)  7.31 us
  transfers between devices with their start and end apart: 8, of which 4 were waited for; matrix products, arithmetic and copies ran while one was open for 16% of the time, Pallas kernels for 0%

profile of v1, /device:TPU:96, one launch (start us, length us, event | category | flops | bytes accessed | tf_op | source)
XLA Modules:
  0.0 286.4 jit_solution(8515371719553929535)
XLA Ops:
  7.6 21.4 %all_to_all.55 = bf16[16,3,5,1280]{3,1,2,0:T(4,128)(2,1)S(1)} all-to-all(bf16[16,3,5,1280]{3,1,2,0:T(4,128)(2,1)S(1)} %broadcast_in_dim.8), channel_id=1, replica_groups=mesh['dp'=16,'frame_0'=4,'frame_1'=4] {'frame_0','frame_1'}, dimensions={0} | all-to-all | bytes 1228800 | tf_op jit(solution)/shard_map/all_to_all | solution.py:25
  30.1 18.5 %all_to_all.56 = bf16[16,5,3840]{2,1,0:T(8,128)(2,1)S(1)} all-to-all(bf16[16,5,3840]{2,1,0:T(8,128)(2,1)S(1)} %broadcast_in_dim.10), channel_id=1, replica_groups=mesh['dp'=16,'frame_0'=4,'frame_1'=4] {'frame_0','frame_1'}, dimensions={0} | all-to-all | bytes 1228800 | tf_op jit(solution)/shard_map/all_to_all | solution.py:25
  48.5 1.1 reshape.189
  49.7 1.0 broadcast_in_dim.9
  50.7 7.8 %all-to-all-start.1 = ((bf16[16,20,1280]{2,1,0:T(8,128)(2,1)}), bf16[16,20,1280]{2,1,0:T(8,128)(2,1)S(1)}, u32[]{:S(2)}, u32[]{:S(2)}) async-start(bf16[16,20,1280]{2,1,0:T(8,128)(2,1)} %broadcast_in_dim.9), calls=%async_computation.1 | async-start | bytes 1966080 | tf_op jit(solution)/shard_map/all_to_all | solution.py:25
  58.8 9.2 %psum.28 = f32[1,32]{1,0:T(1,128)S(1)} all-reduce(f32[1,32]{1,0:T(1,128)S(1)} %bitcast.80), channel_id=1, replica_groups=mesh['dp'=16,'frame_0'=4,'frame_1'=4] {'frame_0'}, use_global_device_ids=true, to_apply=%region_2.0 | all-reduce | flops 32 | bytes 256 | tf_op jit(solution)/shard_map/psum | solution.py:35
  68.0 8.3 %psum.29 = f32[1,32]{1,0:T(1,128)S(1)} all-reduce(f32[1,32]{1,0:T(1,128)S(1)} %psum.28), channel_id=1, replica_groups=mesh['dp'=16,'frame_0'=4,'frame_1'=4] {'frame_1'}, use_global_device_ids=true, to_apply=%region_3.0 | all-reduce | flops 32 | bytes 256 | tf_op jit(solution)/shard_map/psum | solution.py:35
  76.9 8.6 %psum.30 = f32[1,32]{1,0:T(1,128)S(1)} all-reduce(f32[1,32]{1,0:T(1,128)S(1)} %bitcast.79), channel_id=1, replica_groups=mesh['dp'=16,'frame_0'=4,'frame_1'=4] {'frame_0'}, use_global_device_ids=true, to_apply=%region_6.7 | all-reduce | flops 32 | bytes 256 | tf_op jit(solution)/shard_map/psum | solution.py:35
  85.5 8.9 %psum.31 = f32[1,32]{1,0:T(1,128)S(1)} all-reduce(f32[1,32]{1,0:T(1,128)S(1)} %psum.30), channel_id=1, replica_groups=mesh['dp'=16,'frame_0'=4,'frame_1'=4] {'frame_1'}, use_global_device_ids=true, to_apply=%region_7.8 | all-reduce | flops 32 | bytes 256 | tf_op jit(solution)/shard_map/psum | solution.py:35
  95.0 2.9 %collective-permute-start = (bf16[1,1,128,1280]{3,2,1,0:T(8,128)(2,1)S(1)}, bf16[1,1,128,1280]{3,2,1,0:T(8,128)(2,1)S(1)}, u32[]{:S(2)}, u32[]{:S(2)}) collective-permute-start(bf16[1,1,128,1280]{3,2,1,0:T(8,128)(2,1)S(1)} %get-tuple-element.12), channel_id=1, source_target_pairs={{0,1},{1,2},{2,3},{3,4},{4,5},{5,6},{6,7},{7,8},{8,9},{9,10},{10,1... | collective-permute-start | bytes 983048 | tf_op jit(solution)/shard_map/ppermute | solution.py:45
  98.0 1.3 collective-permute-start.1
  100.1 2.5 collective-permute-done
  102.5 4.4 %collective-permute-done.1 = bf16[1,1,128,1280]{3,2,1,0:T(8,128)(2,1)S(1)} collective-permute-done((bf16[1,1,128,1280]{3,2,1,0:T(8,128)(2,1)S(1)}, bf16[1,1,128,1280]{3,2,1,0:T(8,128)(2,1)S(1)}, u32[]{:S(2)}, u32[]{:S(2)}) %collective-permute-start.1) | collective-permute-done | bytes 327712 | tf_op jit(solution)/shard_map/ppermute | solution.py:46
  106.9 1.2 pad_maximum_fusion.1
  108.9 7.5 %all-to-all-start.5 = ((bf16[16,5,1280]{2,1,0:T(8,128)(2,1)}), bf16[16,5,1280]{2,1,0:T(8,128)(2,1)S(1)}, u32[]{:S(2)}, u32[]{:S(2)}) async-start(bf16[16,5,1280]{2,1,0:T(8,128)(2,1)} %broadcast_in_dim.11), calls=%async_computation.5 | async-start | bytes 655360 | tf_op jit(solution)/shard_map/all_to_all | solution.py:25
  116.8 3.2 %fusion.1 = f32[256,1280]{1,0:T(8,128)S(1)} fusion(bf16[256,1280]{1,0:T(8,128)(2,1)} %bitcast.76, bf16[3,1280,1280]{2,1,0:T(8,128)(2,1)} %all-gather.3.cloned.1.call-done), kind=kOutput, calls=%fused_computation.3 | convolution fusion | flops 838860800 | bytes 5242880 | tf_op jit(solution)/shard_map/dot_general | solution.py:80
  120.0 3.0 %fusion.2 = f32[256,1280]{1,0:T(8,128)S(1)} fusion(bf16[256,1280]{1,0:T(8,128)(2,1)S(1)} %bitcast.70, bf16[3,1280,1280]{2,1,0:T(8,128)(2,1)} %all-gather.3.cloned.1.call-done), kind=kOutput, calls=%fused_computation.5 | convolution fusion | flops 838860800 | bytes 5242880 | tf_op jit(solution)/shard_map/dot_general | solution.py:80
  123.0 3.4 %fusion.5 = f32[256,1280]{1,0:T(8,128)S(1)} fusion(f32[256,1280]{1,0:T(8,128)S(1)} %fusion.1, f32[256,1280]{1,0:T(8,128)S(1)} %fusion.2, bf16[256,1280]{1,0:T(8,128)(2,1)S(1)} %bitcast.75, bf16[3,1280,1280]{2,1,0:T(8,128)(2,1)} %all-gather.3.cloned.1.call-done), kind=kOutput, calls=%fused_computation.9 | convolution fusion | flops 839516160 | bytes 7864320 | tf_op jit(solution)/shard_map/dot_general | solution.py:80
  127.3 1.5 copy.42
  128.8 7.0 %all-to-all-start.2 = ((bf16[1,2,128,1280]{3,1,0,2:T(2,128)(2,1)}), bf16[1,2,128,1280]{3,1,0,2:T(2,128)(2,1)S(1)}, u32[]{:S(2)}, u32[]{:S(2)}) async-start(bf16[1,2,128,1280]{3,1,0,2:T(2,128)(2,1)} %copy.42), calls=%async_computation.2 | async-start | bytes 1310720 | tf_op jit(solution)/shard_map/all_to_all | solution.py:114
  136.0 10.7 %all-to-all-done.2 = bf16[1,2,128,1280]{3,1,0,2:T(2,128)(2,1)S(1)} async-done(((bf16[1,2,128,1280]{3,1,0,2:T(2,128)(2,1)}), bf16[1,2,128,1280]{3,1,0,2:T(2,128)(2,1)S(1)}, u32[]{:S(2)}, u32[]{:S(2)}) %all-to-all-start.2) | async-done | bytes 655392 | tf_op jit(solution)/shard_map/all_to_all | solution.py:114
  146.7 1.9 stack.3
  148.6 7.3 %all-to-all-start.6 = ((bf16[16,80,1280]{2,1,0:T(8,128)(2,1)}), bf16[16,80,1280]{2,1,0:T(8,128)(2,1)}, u32[]{:S(2)}, u32[]{:S(2)}) async-start(bf16[16,80,1280]{2,1,0:T(8,128)(2,1)} %stack.3), calls=%async_computation.6 | async-start | bytes 6553600 | tf_op jit(solution)/shard_map/all_to_all | solution.py:130
  156.0 63.8 %all-gather.5.cloned.1.call-done = bf16[1280,3840]{1,0:T(8,128)(2,1)} async-done(((bf16[80,3840]{1,0:T(8,128)(2,1)}), bf16[1280,3840]{1,0:T(8,128)(2,1)}) %all-gather.5.cloned.1.call-update) | async-done | bytes 9830416 | tf_op jit(solution)/shard_map/all_gather | solution.py:118
  219.8 6.5 %convolution_convert_fusion = bf16[256,3840]{1,0:T(8,128)(2,1)S(1)} fusion(bf16[256,1280]{1,0:T(8,128)(2,1)S(1)} %bitcast.77, bf16[1280,3840]{1,0:T(8,128)(2,1)} %all-gather.5.cloned.1.call-done), kind=kOutput, calls=%fused_computation.1 | convolution fusion | flops 2517565440 | bytes 12451840 | tf_op jit(solution)/shard_map/dot_general | solution.py:80
  226.3 4.5 %reshape_reshape.3 = bf16[1,32,8,3,20,64]{5,4,3,2,1,0:T(8,128)(2,1)} reshape(bf16[256,3840]{1,0:T(8,128)(2,1)S(1)} %convolution_convert_fusion) | data formatting | bytes 3932160 | tf_op jit(solution)/shard_map/reshape;reshape | solution.py:62
  230.7 3.3 %fusion.28 = (bf16[1,32,8,1,20,64]{5,4,3,2,1,0:T(8,128)(2,1)S(1)}, bf16[1,32,8,1,20,64]{5,4,3,2,1,0:T(8,128)(2,1)S(1)}, bf16[1,32,8,1,20,64]{5,4,3,2,1,0:T(8,128)(2,1)S(1)}) fusion(bf16[1,32,8,3,20,64]{5,4,3,2,1,0:T(8,128)(2,1)} %reshape_reshape.3), kind=kLoop, calls=%fused_computation.55 | loop fusion | bytes 3932160 | tf_op jit(solution)/shard_map/slice | solution.py:65
  234.0 1.7 fusion.21
  235.7 6.0 %fusion.30 = (f32[8,20,32]{2,1,0:T(8,128)S(1)}, f32[8,20,32,32]{2,3,1,0:T(8,128)S(1)}) fusion(f32[8,20,32,32]{2,3,1,0:T(8,128)S(1)} %fusion.21), kind=kOutput, calls=%fused_computation.57 | output fusion | flops 655391 | bytes 1331200 | tf_op jit(solution)/shard_map/sub | solution.py:70
  241.7 1.2 fusion.15
  244.4 31.3 %all_to_all.57 = bf16[1,32,8,1280]{3,2,0,1:T(8,128)(2,1)S(1)} all-to-all(bf16[1,32,8,1280]{3,2,0,1:T(8,128)(2,1)S(1)} %bitcast.74), channel_id=1, replica_groups=mesh['dp'=16,'frame_0'=4,'frame_1'=4] {'frame_0','frame_1'}, dimensions={1} | all-to-all | bytes 1310720 | tf_op jit(solution)/shard_map/all_to_all | solution.py:76
  275.8 3.8 %fusion.7 = bf16[1,2,128,1280]{3,2,1,0:T(8,128)(2,1)} fusion(bf16[1280,1280,1]{1,0,2:T(8,128)(2,1)} %bitcast.27, bf16[1,2,128,1280]{3,2,1,0:T(8,128)(2,1)S(1)} %get-tuple-element.6, bf16[1,2,16,8,1280]{4,3,1,2,0:T(8,128)(2,1)S(1)} %bitcast.78), kind=kOutput, calls=%fused_computation.14 | convolution fusion | flops 839843840 | bytes 5242880 | tf_op jit(solution)/shard_map/dot_general | solution.py:80
  (53 shorter events, 7.5 us)
Async XLA Ops:
  6.5 110.3 %all-gather.3.cloned.1.call-start = ((), (), s32[]{:S(2)}) async-start(), calls=%async_computation.7 | async-start | bytes 10444800 | tf_op jit(solution)/shard_map/all_gather | solution.py:103
  7.6 22.4 %copy-start.2 = (bf16[5,3840]{1,0:T(8,128)(2,1)S(1)}, bf16[5,3840]{1,0:T(8,128)(2,1)}, u32[]{:S(2)}) copy-start(bf16[5,3840]{1,0:T(8,128)(2,1)} %param.12) | copy-start | bytes 115204
  29.9 189.8 %all-gather.5.cloned.1.call-start = ((), (), s32[]{:S(2)}) async-start(), calls=%async_computation.8 | async-start | bytes 10444800 | tf_op jit(solution)/shard_map/all_gather | solution.py:118
  48.5 1.1 copy-start.3
  49.7 8.9 %copy-start = (bf16[1,2,128,1280]{3,2,1,0:T(8,128)(2,1)S(1)}, bf16[1,2,128,1280]{3,2,1,0:T(8,128)(2,1)}, u32[]{:S(2)}) copy-start(bf16[1,2,128,1280]{3,2,1,0:T(8,128)(2,1)} %param.7) | copy-start | bytes 1966084
  50.7 43.8 %copy-start.5 = (f32[1280]{0:T(1024)S(1)}, f32[1280]{0:T(1024)}, u32[]{:S(2)}) copy-start(f32[1280]{0:T(1024)} %param.9) | copy-start | bytes 15364
  50.7 57.4 %all-to-all-start.1 = ((bf16[16,20,1280]{2,1,0:T(8,128)(2,1)}), bf16[16,20,1280]{2,1,0:T(8,128)(2,1)S(1)}, u32[]{:S(2)}, u32[]{:S(2)}) async-start(bf16[16,20,1280]{2,1,0:T(8,128)(2,1)} %broadcast_in_dim.9), calls=%async_computation.1 | async-start | bytes 1966080 | tf_op jit(solution)/shard_map/all_to_all | solution.py:25
  95.0 13.1 %copy-start.4 = (bf16[5,1280]{1,0:T(8,128)(2,1)S(1)}, bf16[5,1280]{1,0:T(8,128)(2,1)}, u32[]{:S(2)}) copy-start(bf16[5,1280]{1,0:T(8,128)(2,1)} %param.13) | copy-start | bytes 38404
  95.0 7.5 %collective-permute-start = (bf16[1,1,128,1280]{3,2,1,0:T(8,128)(2,1)S(1)}, bf16[1,1,128,1280]{3,2,1,0:T(8,128)(2,1)S(1)}, u32[]{:S(2)}, u32[]{:S(2)}) collective-permute-start(bf16[1,1,128,1280]{3,2,1,0:T(8,128)(2,1)S(1)} %get-tuple-element.12), channel_id=1, source_target_pairs={{0,1},{1,2},{2,3},{3,4},{4,5},{5,6},{6,7},{7,8},{8,9},{9,10},{10,1... | collective-permute-start | bytes 983048 | tf_op jit(solution)/shard_map/ppermute | solution.py:45
  98.0 9.0 %collective-permute-start.1 = (bf16[1,1,128,1280]{3,2,1,0:T(8,128)(2,1)S(1)}, bf16[1,1,128,1280]{3,2,1,0:T(8,128)(2,1)S(1)}, u32[]{:S(2)}, u32[]{:S(2)}) collective-permute-start(bf16[1,1,128,1280]{3,2,1,0:T(8,128)(2,1)S(1)} %get-tuple-element.13), channel_id=1, source_target_pairs={{1,0},{2,1},{3,2},{4,3},{5,4},{6,5},{7,6},{8,7},{9,8},{10,9},{11,1... | collective-permute-start | bytes 983048 | tf_op jit(solution)/shard_map/ppermute | solution.py:46
  108.9 20.0 %all-to-all-start.5 = ((bf16[16,5,1280]{2,1,0:T(8,128)(2,1)}), bf16[16,5,1280]{2,1,0:T(8,128)(2,1)S(1)}, u32[]{:S(2)}, u32[]{:S(2)}) async-start(bf16[16,5,1280]{2,1,0:T(8,128)(2,1)} %broadcast_in_dim.11), calls=%async_computation.5 | async-start | bytes 655360 | tf_op jit(solution)/shard_map/all_to_all | solution.py:25
  120.0 3.0 %copy-start.1 = (bf16[1,2,128,1280]{3,2,1,0:T(8,128)(2,1)S(1)}, bf16[1,2,128,1280]{3,2,1,0:T(8,128)(2,1)}, u32[]{:S(2)}) copy-start(bf16[1,2,128,1280]{3,2,1,0:T(8,128)(2,1)} %get-tuple-element.10) | copy-start | bytes 1966084
  128.8 17.8 %all-to-all-start.2 = ((bf16[1,2,128,1280]{3,1,0,2:T(2,128)(2,1)}), bf16[1,2,128,1280]{3,1,0,2:T(2,128)(2,1)S(1)}, u32[]{:S(2)}, u32[]{:S(2)}) async-start(bf16[1,2,128,1280]{3,1,0,2:T(2,128)(2,1)} %copy.42), calls=%async_computation.2 | async-start | bytes 1310720 | tf_op jit(solution)/shard_map/all_to_all | solution.py:114
  148.6 95.9 %all-to-all-start.6 = ((bf16[16,80,1280]{2,1,0:T(8,128)(2,1)}), bf16[16,80,1280]{2,1,0:T(8,128)(2,1)}, u32[]{:S(2)}, u32[]{:S(2)}) async-start(bf16[16,80,1280]{2,1,0:T(8,128)(2,1)} %stack.3), calls=%async_computation.6 | async-start | bytes 6553600 | tf_op jit(solution)/shard_map/all_to_all | solution.py:130
Sparse Core Ops, SparseCore 0:
  30.0 81.5 all-gather.2
  113.5 106.2 all-gather.4
